TPU v7x, 128 devices: a whole 4x4x4 slice. The times are simulated.
128 devices in a mesh: band: 8 (over y_lo, z), dom: 16 (over x, y_hi, core).
Axes of the slice: x: 4, y: 4 (y_hi: 2, y_lo: 2; y = y_hi * 2 + y_lo), z: 4, core: 2. Of those that a mesh axis runs over, the one named last changes fastest.
Arguments:
- orbitals: bfloat16 [64, 32, 128, 256], P('band', 'dom'), may hold values from -6 to 6
- visit_blocks: int32 [2], replicated, may hold values from 0 to 15, as said below
- kernel_rates: float32 [3], replicated, may hold values from 0.0098 to 3.41
- kernel_weights: float32 [3], replicated, may hold values from 0.07 to 1.42
Outputs:
- exchange_terms: float32 [64, 32, 128, 256], P('band', 'dom')
Inputs may be any that keep to these rules, and one draw needn't show every extreme that they name: Entry k names band group visit_blocks[k] // 2 and the half visit_blocks[k] % 2 of its orbitals; the entries are distinct, and one of them names the second half of the last band group.
All inputs are finite; a program needn't handle non-finite values.
Results may differ from a plain program's by a relative error of at most 0.0023.
Values may be sent and summed in bfloat16 or wider, within the bound.
A program may use at most 192 MiB of HBM per device.

v0:
```python
import jax
import jax.numpy as jnp
from jax import lax
from jax.experimental import pallas as pl
from jax.experimental.pallas import tpu as pltpu
from jax.sharding import PartitionSpec as P

BLOCK = 4
VISITS = 2
REACH = 2
GAUSS = 3
CHUNK = 16


def tap_values(rate):
    lane = lax.broadcasted_iota(jnp.int32, (8, 128), 1).astype(jnp.float32)
    scale = 1.0 + lane * (1.0 / 128.0)
    near = jnp.exp(jnp.full((8, 128), -rate))
    far = jnp.exp(jnp.full((8, 128), -4.0 * rate))
    near_error = scale * near - (scale * near).astype(jnp.bfloat16).astype(jnp.float32)
    far_error = scale * far - (scale * far).astype(jnp.bfloat16).astype(jnp.float32)
    cost = (near_error * near_error + far_error * far_error) / (scale * scale)
    best = jnp.min(jnp.where(cost == jnp.min(cost), scale, 4.0))
    return jnp.max(near), jnp.max(far), best


def banded(size, block, scale, near, far):
    row = lax.broadcasted_iota(jnp.int32, (size, size), 0)
    column = lax.broadcasted_iota(jnp.int32, (size, size), 1)
    gap = jnp.abs(row - column)
    taps = jnp.where(gap == 0, scale, jnp.where(gap == 1, scale * near, scale * far))
    keep = gap <= REACH
    if block < size:
        keep = keep & ((row // block) == (column // block))
    return jnp.where(keep, taps, 0.0).astype(jnp.bfloat16)


def pair_kernel(rates, weights, own, low, high, v_own, v_low, v_high, out, lines, y_band, z_band):
    residents, planes, cy, cz = own.shape
    taps = []
    for g in range(GAUSS):
        near, far, scale = tap_values(rates[g])
        taps.append((near, far, weights[g] / (scale * scale)))
        y_band[g] = banded(planes * cy, cy, scale, near, far)
        z_band[g * cz : (g + 1) * cz, :] = banded(cz, cz, scale, near, far)
    out[...] = jnp.zeros_like(out)
    sides = ((low, v_low, 0), (low, v_low, 1), (own, v_own, 0), (own, v_own, 1), (high, v_high, 0), (high, v_high, 1))

    def x_pass(i, j):
        for y in range(0, cy, CHUNK):
            rows = slice(y, y + CHUNK)
            density = [(r[i, p, rows, :] * v[j, p, rows, :]).astype(jnp.float32) for r, v, p in sides]
            for p in range(planes):
                ones = density[p + 1] + density[p + 3]
                twos = density[p] + density[p + 4]
                for g in range(GAUSS):
                    near, far, _ = taps[g]
                    line = density[p + 2] + near * ones + far * twos
                    lines[i, g, p * cy + y : p * cy + y + CHUNK, :] = line.astype(jnp.bfloat16)

    def yz_pass(i, j):
        along = []
        for g in range(GAUSS):
            line = jnp.dot(y_band[g], lines[i, g], preferred_element_type=jnp.float32)
            along.append((line * taps[g][2]).astype(jnp.bfloat16))
        potential = jnp.dot(jnp.concatenate(along, axis=1), z_band[...], preferred_element_type=jnp.float32)
        for p in range(planes):
            out[i, p] += potential[p * cy : (p + 1) * cy] * v_own[j, p].astype(jnp.float32)

    def visitor(j, carry):
        for i in range(residents):
            x_pass(i, j)
            yz_pass(i, j)
        return carry

    lax.fori_loop(0, v_own.shape[0], visitor, 0)


def pairs(rates, weights, *blocks):
    residents, planes, cy, cz = blocks[0].shape
    vmem = pl.BlockSpec(memory_space=pltpu.VMEM)
    smem = pl.BlockSpec(memory_space=pltpu.SMEM)
    return pl.pallas_call(
        pair_kernel,
        out_shape=jax.ShapeDtypeStruct(blocks[0].shape, jnp.float32),
        in_specs=[smem, smem] + [vmem] * 6,
        out_specs=vmem,
        scratch_shapes=[
            pltpu.VMEM((residents, GAUSS, planes * cy, cz), jnp.bfloat16),
            pltpu.VMEM((GAUSS, planes * cy, planes * cy), jnp.bfloat16),
            pltpu.VMEM((GAUSS * cz, cz), jnp.bfloat16),
        ],
        compiler_params=pltpu.CompilerParams(vmem_limit_bytes=48 << 20),
    )(rates, weights, *blocks)


def neighbours(block):
    count = lax.axis_size("dom")
    forward = [(i, i + 1) for i in range(count - 1)]
    backward = [(target, source) for source, target in forward]
    return lax.ppermute(block, "dom", forward), lax.ppermute(block, "dom", backward)


def local(orbitals, visit_blocks, kernel_rates, kernel_weights):
    low, high = neighbours(orbitals)
    picked = []
    for visit_index in range(VISITS):
        code = visit_blocks[visit_index]
        own_block = lax.dynamic_slice_in_dim(orbitals, code % 2 * BLOCK, BLOCK, 0)
        picked.append(jnp.where(lax.axis_index("band") == code // 2, own_block, 0).astype(orbitals.dtype))
    visitors = lax.psum(jnp.concatenate(picked, 0), "band")
    v_low, v_high = neighbours(visitors)
    return pairs(kernel_rates, kernel_weights, orbitals, low, high, visitors, v_low, v_high)


def solution(mesh):
    return jax.shard_map(
        local,
        mesh=mesh,
        in_specs=(P("band", "dom", None, None), P(), P(), P()),
        out_specs=P("band", "dom", None, None),
        check_vma=False,
    )
```

profile of v0, /device:TPU:3, one launch (start us, length us, event | category | flops | bytes accessed | tf_op | source)
XLA Modules:
  0.0 166.5 jit_solution(5009447417966016010)
XLA Ops:
  6.5 0.0 all-reduce.2.cloned.1.call-start
  6.5 1.4 fusion
  13.0 1.3 dynamic-slice_select_fusion.1
  14.3 0.0 copy-start
  14.3 0.0 copy-start.2
  14.4 0.0 copy-start.3
  14.4 1.1 pad_maximum_fusion
  15.4 0.0 all-reduce.2.cloned.1.call-update
  15.5 0.5 copy-done
  15.9 2.6 %collective-permute-start.1 = (bf16[8,2,128,256]{3,2,1,0:T(8,128)(2,1)S(1)}, bf16[8,2,128,256]{3,2,1,0:T(8,128)(2,1)S(1)}, u32[]{:S(2)}, u32[]{:S(2)}) collective-permute-start(bf16[8,2,128,256]{3,2,1,0:T(8,128)(2,1)S(1)} %copy-done), channel_id=1, source_target_pairs={{1,0},{2,1},{3,2},{4,3},{5,4},{6,5},{7,6},{8,7},{9,8},{10,9},{11,1... | collective-permute-start | bytes 3145736 | tf_op jit(solution)/shard_map/ppermute | solution.py:101
  18.5 4.7 %collective-permute-start = (bf16[8,2,128,256]{3,2,1,0:T(8,128)(2,1)S(1)}, bf16[8,2,128,256]{3,2,1,0:T(8,128)(2,1)S(1)}, u32[]{:S(2)}, u32[]{:S(2)}) collective-permute-start(bf16[8,2,128,256]{3,2,1,0:T(8,128)(2,1)S(1)} %copy-done), channel_id=1, source_target_pairs={{0,1},{1,2},{2,3},{3,4},{4,5},{5,6},{6,7},{7,8},{8,9},{9,10},{10,1... | collective-permute-start | bytes 3145736 | tf_op jit(solution)/shard_map/ppermute | solution.py:101
  23.2 78.1 %all-reduce.2.cloned.1.call-done.v_own = bf16[8,2,128,256]{3,2,1,0:T(8,128)(2,1)} async-done(((bf16[8,2,128,256]{3,2,1,0:T(8,128)(2,1)}), bf16[8,2,128,256]{3,2,1,0:T(8,128)(2,1)}) %all-reduce.2.cloned.1.call-update) | async-done | bytes 1048592 | tf_op jit(solution)/shard_map/psum | solution.py:111
  101.4 7.6 %collective-permute-start.3 = (bf16[8,2,128,256]{3,2,1,0:T(8,128)(2,1)}, bf16[8,2,128,256]{3,2,1,0:T(8,128)(2,1)S(1)}, u32[]{:S(2)}, u32[]{:S(2)}) collective-permute-start(bf16[8,2,128,256]{3,2,1,0:T(8,128)(2,1)} %all-reduce.2.cloned.1.call-done.v_own), channel_id=1, source_target_pairs={{1,0},{2,1},{3,2},{4,3},{5,4},{6,5},{7,6},{8,7},{9,8},{10,9},{11,1... | collective-permute-start | bytes 3145736 | tf_op jit(solution)/shard_map/ppermute | solution.py:101
  109.0 4.2 %collective-permute-start.2 = (bf16[8,2,128,256]{3,2,1,0:T(8,128)(2,1)}, bf16[8,2,128,256]{3,2,1,0:T(8,128)(2,1)S(1)}, u32[]{:S(2)}, u32[]{:S(2)}) collective-permute-start(bf16[8,2,128,256]{3,2,1,0:T(8,128)(2,1)} %all-reduce.2.cloned.1.call-done.v_own), channel_id=1, source_target_pairs={{0,1},{1,2},{2,3},{3,4},{4,5},{5,6},{6,7},{7,8},{8,9},{9,10},{10,1... | collective-permute-start | bytes 3145736 | tf_op jit(solution)/shard_map/ppermute | solution.py:101
  113.2 0.0 collective-permute-done.1.high
  113.2 0.0 collective-permute-done.low
  113.2 22.0 %collective-permute-done.3.v_high = bf16[8,2,128,256]{3,2,1,0:T(8,128)(2,1)S(1)} collective-permute-done((bf16[8,2,128,256]{3,2,1,0:T(8,128)(2,1)}, bf16[8,2,128,256]{3,2,1,0:T(8,128)(2,1)S(1)}, u32[]{:S(2)}, u32[]{:S(2)}) %collective-permute-start.3) | collective-permute-done | bytes 1048608 | tf_op jit(solution)/shard_map/ppermute | solution.py:101
  135.2 0.0 copy-start.4
  135.2 0.0 collective-permute-done.2.v_low
  135.2 1.0 copy-done.4
  136.2 0.0 copy-done.2
  136.2 0.0 copy-done.3
  136.2 0.0 copy-start.1
  136.2 1.2 copy-done.1
  137.4 22.2 %shard_map.46 = f32[8,2,128,256]{3,2,1,0:T(8,128)} custom-call(f32[3]{0:T(128)S(1)} %copy-done.2, f32[3]{0:T(128)S(1)} %copy-done.3, bf16[8,2,128,256]{3,2,1,0:T(8,128)(2,1)S(1)} %copy-done, bf16[8,2,128,256]{3,2,1,0:T(8,128)(2,1)S(1)} %collective-permute-done.low, bf16[8,2,128,256]{3,2,1,0:T(8,128)(2,1)S(1)} %collective-permute-done.1.high, ...), custom_call_target="tpu_custom_call" | custom-call | tf_op jit(solution)/shard_map/pallas_call | solution.py:83
Async XLA Ops:
  6.5 94.8 %all-reduce.2.cloned.1.call-start = ((), (), s32[]{:S(2)}) async-start(), calls=%async_computation | async-start | bytes 2097152 | tf_op jit(solution)/shard_map/psum | solution.py:111
  14.3 1.6 copy-start
  14.3 121.9 %copy-start.2 = (f32[3]{0:T(128)S(1)}, f32[3]{0:T(128)}, u32[]{:S(2)}) copy-start(f32[3]{0:T(128)} %rates.1) | copy-start | bytes 40
  14.4 121.9 %copy-start.3 = (f32[3]{0:T(128)S(1)}, f32[3]{0:T(128)}, u32[]{:S(2)}) copy-start(f32[3]{0:T(128)} %weights.1) | copy-start | bytes 40
  15.9 97.3 %collective-permute-start.1 = (bf16[8,2,128,256]{3,2,1,0:T(8,128)(2,1)S(1)}, bf16[8,2,128,256]{3,2,1,0:T(8,128)(2,1)S(1)}, u32[]{:S(2)}, u32[]{:S(2)}) collective-permute-start(bf16[8,2,128,256]{3,2,1,0:T(8,128)(2,1)S(1)} %copy-done), channel_id=1, source_target_pairs={{1,0},{2,1},{3,2},{4,3},{5,4},{6,5},{7,6},{8,7},{9,8},{10,9},{11,1... | collective-permute-start | bytes 3145736 | tf_op jit(solution)/shard_map/ppermute | solution.py:101
  18.5 94.7 %collective-permute-start = (bf16[8,2,128,256]{3,2,1,0:T(8,128)(2,1)S(1)}, bf16[8,2,128,256]{3,2,1,0:T(8,128)(2,1)S(1)}, u32[]{:S(2)}, u32[]{:S(2)}) collective-permute-start(bf16[8,2,128,256]{3,2,1,0:T(8,128)(2,1)S(1)} %copy-done), channel_id=1, source_target_pairs={{0,1},{1,2},{2,3},{3,4},{4,5},{5,6},{6,7},{7,8},{8,9},{9,10},{10,1... | collective-permute-start | bytes 3145736 | tf_op jit(solution)/shard_map/ppermute | solution.py:101
  101.4 33.9 %collective-permute-start.3 = (bf16[8,2,128,256]{3,2,1,0:T(8,128)(2,1)}, bf16[8,2,128,256]{3,2,1,0:T(8,128)(2,1)S(1)}, u32[]{:S(2)}, u32[]{:S(2)}) collective-permute-start(bf16[8,2,128,256]{3,2,1,0:T(8,128)(2,1)} %all-reduce.2.cloned.1.call-done.v_own), channel_id=1, source_target_pairs={{1,0},{2,1},{3,2},{4,3},{5,4},{6,5},{7,6},{8,7},{9,8},{10,9},{11,1... | collective-permute-start | bytes 3145736 | tf_op jit(solution)/shard_map/ppermute | solution.py:101
  109.0 26.2 %collective-permute-start.2 = (bf16[8,2,128,256]{3,2,1,0:T(8,128)(2,1)}, bf16[8,2,128,256]{3,2,1,0:T(8,128)(2,1)S(1)}, u32[]{:S(2)}, u32[]{:S(2)}) collective-permute-start(bf16[8,2,128,256]{3,2,1,0:T(8,128)(2,1)} %all-reduce.2.cloned.1.call-done.v_own), channel_id=1, source_target_pairs={{0,1},{1,2},{2,3},{3,4},{4,5},{5,6},{6,7},{7,8},{8,9},{9,10},{10,1... | collective-permute-start | bytes 3145736 | tf_op jit(solution)/shard_map/ppermute | solution.py:101
  135.2 1.0 copy-start.4
  136.2 1.2 copy-start.1
Sparse Core Ops, SparseCore 0:
  15.6 85.7 all-reduce.1
where the time goes:
time: 167 us
  waiting for transfers between devices  100 us (60%)
  Pallas kernels  22.2 us (13%)
  starting transfers between devices  19.1 us (11%)
  between operations  18.6 us (11%)
  local copies, waits for them, and re-layouts  4.1 us (2%)
  other arithmetic  2.34 us (1%)
    psum x1, waiting for transfers between devices, local(): visitors = lax.psum(jnp.concatenate(picked, 0), 'band')  78.1 us
    pallas_call x1, Pallas kernels, pairs(): pl.pallas_call(pair_kernel, out_shape=jax.ShapeDtypeStruct(blocks[0].shap...  22.2 us
    ppermute x2, waiting for transfers between devices, neighbours(): lax.ppermute(block, 'dom', backward)  22 us
    ppermute x2, starting transfers between devices, neighbours(): lax.ppermute(block, 'dom', backward)  10.2 us
    ppermute x2, starting transfers between devices, neighbours(): lax.ppermute(block, 'dom', forward)  8.96 us
  transfers between devices with their start and end apart: 5, of which 2 were waited for; matrix products, arithmetic and copies ran while one was open for 0% of the time, Pallas kernels for 0%

commit v1 on v0

--- a/solution.py
+++ b/solution.py
@@ -1,3 +1,5 @@
+import functools
+
 import jax
 import jax.numpy as jnp
 from jax import lax
@@ -9,6 +11,11 @@
 VISITS = 2
 REACH = 2
 GAUSS = 3
+RING = 4
+LAST_OWNER = 7
+CROSS = (0, 1, 3, 2)
+EARLY = 2
+MESH = pl.DeviceIdType.MESH
 CHUNK = 16
 
 
@@ -35,7 +42,7 @@
     return jnp.where(keep, taps, 0.0).astype(jnp.bfloat16)
 
 
-def pair_kernel(rates, weights, own, low, high, v_own, v_low, v_high, out, lines, y_band, z_band):
+def pair_kernel(rates, weights, own, off, par, v_own, v_off, v_par, out, lines, y_band, z_band):
     residents, planes, cy, cz = own.shape
     taps = []
     for g in range(GAUSS):
@@ -44,7 +51,9 @@
         y_band[g] = banded(planes * cy, cy, scale, near, far)
         z_band[g * cz : (g + 1) * cz, :] = banded(cz, cz, scale, near, far)
     out[...] = jnp.zeros_like(out)
-    sides = ((low, v_low, 0), (low, v_low, 1), (own, v_own, 0), (own, v_own, 1), (high, v_high, 0), (high, v_high, 1))
+    flip = lax.axis_index("dom") % 2
+    plane = (flip, 1 - flip)
+    sides = [(r, v, plane[p]) for r, v in ((off, v_off), (own, v_own), (par, v_par)) for p in range(planes)]
 
     def x_pass(i, j):
         for y in range(0, cy, CHUNK):
@@ -65,7 +74,7 @@
             along.append((line * taps[g][2]).astype(jnp.bfloat16))
         potential = jnp.dot(jnp.concatenate(along, axis=1), z_band[...], preferred_element_type=jnp.float32)
         for p in range(planes):
-            out[i, p] += potential[p * cy : (p + 1) * cy] * v_own[j, p].astype(jnp.float32)
+            out[i, plane[p]] += potential[p * cy : (p + 1) * cy] * v_own[j, plane[p]].astype(jnp.float32)
 
     def visitor(j, carry):
         for i in range(residents):
@@ -94,23 +103,175 @@
     )(rates, weights, *blocks)
 
 
-def neighbours(block):
-    count = lax.axis_size("dom")
-    forward = [(i, i + 1) for i in range(count - 1)]
-    backward = [(target, source) for source, target in forward]
-    return lax.ppermute(block, "dom", forward), lax.ppermute(block, "dom", backward)
+def exchange_kernel(owner, orbitals, other, off, par, v_own, v_off, v_par, unit_send, own_recv, off_recv, par_recv,
+                    r_send, r_off_recv, r_par_recv, local_sem):
+    band, dom = lax.axis_index("band"), lax.axis_index("dom")
+    side, place, core = band // RING, band % RING, dom % 2
+    up = side * RING + (place + 1) % RING
+    down = side * RING + (place + RING - 1) % RING
+    twin = (1 - side) * RING + place
+    mate = dom + 1 - 2 * core
+    away = dom - 1 + 2 * core
+    inside = (dom > 0) & (dom < lax.axis_size("dom") - 1)
+    yes = dom >= 0
+
+    barrier = pltpu.get_barrier_semaphore()
+    for target in (up, down, twin):
+        pl.semaphore_signal(barrier, inc=1, device_id={"band": target}, device_id_type=MESH)
+    pl.semaphore_signal(barrier, inc=1, device_id={"dom": mate}, device_id_type=MESH)
+
+    @pl.when(inside)
+    def _():
+        pl.semaphore_signal(barrier, inc=1, device_id={"dom": away}, device_id_type=MESH)
+        pl.semaphore_wait(barrier, 5)
+
+    @pl.when(jnp.logical_not(inside))
+    def _():
+        pl.semaphore_wait(barrier, 4)
+        off[...] = jnp.zeros_like(off)
+        v_off[...] = jnp.zeros_like(v_off)
+
+    def send(source, target, send_sem, recv_sem, **device):
+        return pltpu.make_async_remote_copy(
+            src_ref=source, dst_ref=target, send_sem=send_sem, recv_sem=recv_sem, device_id=device, device_id_type=MESH
+        )
+
+    def routes(block, m, halo):
+        root = (LAST_OWNER, owner)[block]
+        row = block * BLOCK + m
+        gap = (place + RING - root % RING) % RING
+        home = side == root // RING
+        step = (gap - CROSS[m] + RING) % RING
+        climbs = m < BLOCK // 2
+        if climbs:
+            go_up, go_down = home & (gap < 3), None
+        else:
+            go_up, go_down = None, home & (gap != 1)
+        far_up = jnp.logical_not(home) & ((step == 0) | (step == 1) if not halo else step == 0)
+        far_down = jnp.logical_not(home) & (step == 0 if not halo else (step == 0) | (step == 3))
+        go_up = far_up if go_up is None else go_up | far_up
+        go_down = far_down if go_down is None else go_down | far_down
+        buffer, recv = (v_off, off_recv) if halo else (v_own, own_recv)
+        slots = unit_send.at[halo, row]
+        first = band == root
+        source = orbitals.at[BLOCK + m] if block == 0 else other.at[m]
+        plan = []
+        for k, (condition, device) in enumerate(
+            ((go_up, {"band": up}), (go_down, {"band": down}), (home & (gap == CROSS[m]), {"band": twin}))
+        ):
+            if halo:
+                condition = condition & inside
+                plan.append((condition, send(v_off.at[row], v_off.at[row], slots.at[k], recv.at[row], **device)))
+            else:
+                plan.append((condition & first, send(source, v_own.at[row], slots.at[k], recv.at[row], **device)))
+                plan.append(
+                    (condition & jnp.logical_not(first), send(v_own.at[row], v_own.at[row], slots.at[k], recv.at[row], **device))
+                )
+        if not halo:
+            plan.append((first, send(source, v_par.at[row], slots.at[3], par_recv.at[row], dom=mate)))
+            plan.append((jnp.logical_not(first), send(v_own.at[row], v_par.at[row], slots.at[3], par_recv.at[row], dom=mate)))
+            plan.append((first & inside, send(source, v_off.at[row], slots.at[4], off_recv.at[row], dom=away)))
+        return first, source, row, plan
+
+    def start(condition, copy):
+        @pl.when(condition)
+        def _():
+            copy.start()
+
+    def finish(condition, copy):
+        @pl.when(condition)
+        def _():
+            copy.wait_send()
+
+    r_away = [send(orbitals.at[i], off.at[i], r_send.at[0, i], r_off_recv.at[i], dom=away) for i in range(2 * BLOCK)]
+    r_mate = [send(orbitals.at[i], par.at[i], r_send.at[1, i], r_par_recv.at[i], dom=mate) for i in range(2 * BLOCK)]
+    units = [(block, m, halo) for halo in range(2) for m in (0, 2, 1, 3) for block in range(2)]
+    plans = [routes(*unit) for unit in units]
+
+    for (block, m, halo), (first, source, row, plan) in zip(units, plans):
+        if not halo:
+            for condition, copy in plan:
+                pass
+
+            @pl.when(first)
+            def _(source=source, row=row):
+                pltpu.make_async_copy(source, v_own.at[row], local_sem.at[row]).start()
+
+    for (block, m, halo), (first, source, row, plan) in zip(units, plans):
+        if not halo:
+
+            @pl.when(first)
+            def _(plan=plan):
+                for condition, copy in plan:
+                    start(condition, copy)
+
+    for i in range(EARLY):
+        start(inside, r_away[i])
+    for copy in r_mate:
+        copy.start()
+    waiting = list(r_away[EARLY:])
+    for (block, m, halo), (first, source, row, plan) in zip(units, plans):
+        if halo:
+
+            @pl.when(inside)
+            def _(row=row):
+                send(v_off.at[row], v_off.at[row], unit_send.at[1, row, 4], off_recv.at[row], dom=away).wait_recv()
+
+            for condition, copy in plan:
+                start(condition, copy)
+        else:
+
+            @pl.when(jnp.logical_not(first))
+            def _(row=row, plan=plan):
+                send(v_own.at[row], v_own.at[row], unit_send.at[0, row, 0], own_recv.at[row], dom=mate).wait_recv()
+                for condition, copy in plan:
+                    start(condition, copy)
+
+        if waiting:
+            start(inside, waiting.pop(0))
+    for (block, m, halo), (first, source, row, plan) in zip(units, plans):
+        for condition, copy in plan:
+            finish(condition, copy)
+        if not halo:
+            send(v_own.at[row], v_par.at[row], unit_send.at[0, row, 3], par_recv.at[row], dom=mate).wait_recv()
+
+            @pl.when(first)
+            def _(source=source, row=row):
+                pltpu.make_async_copy(source, v_own.at[row], local_sem.at[row]).wait()
+
+    for i in range(2 * BLOCK):
+
+        @pl.when(inside)
+        def _(i=i):
+            r_away[i].wait()
+
+        r_mate[i].wait()
+
+
+def exchange(owner, orbitals, other):
+    vmem = pl.BlockSpec(memory_space=pltpu.VMEM)
+    anywhere = pl.BlockSpec(memory_space=pl.ANY)
+    count = 2 * BLOCK
+    dma = pltpu.SemaphoreType.DMA
+    return pl.pallas_call(
+        functools.partial(exchange_kernel, owner),
+        out_shape=[jax.ShapeDtypeStruct(orbitals.shape, orbitals.dtype)] * 5,
+        in_specs=[anywhere, anywhere],
+        out_specs=[vmem] * 5,
+        scratch_shapes=[dma((2, count, 5)), dma((count,)), dma((count,)), dma((count,)), dma((2, count)), dma((count,)),
+                        dma((count,)), dma((count,))],
+        compiler_params=pltpu.CompilerParams(collective_id=owner, has_side_effects=True, vmem_limit_bytes=16 << 20),
+        name="exchange" + str(owner),
+    )(orbitals, other)
 
 
 def local(orbitals, visit_blocks, kernel_rates, kernel_weights):
-    low, high = neighbours(orbitals)
-    picked = []
-    for visit_index in range(VISITS):
-        code = visit_blocks[visit_index]
-        own_block = lax.dynamic_slice_in_dim(orbitals, code % 2 * BLOCK, BLOCK, 0)
-        picked.append(jnp.where(lax.axis_index("band") == code // 2, own_block, 0).astype(orbitals.dtype))
-    visitors = lax.psum(jnp.concatenate(picked, 0), "band")
-    v_low, v_high = neighbours(visitors)
-    return pairs(kernel_rates, kernel_weights, orbitals, low, high, visitors, v_low, v_high)
+    last = 2 * LAST_OWNER + 1
+    code = jnp.where(visit_blocks[0] == last, visit_blocks[1], visit_blocks[0])
+    other = lax.dynamic_slice_in_dim(orbitals, code % 2 * BLOCK, BLOCK, 0)
+    branches = [functools.partial(exchange, owner) for owner in range(LAST_OWNER + 1)]
+    off, par, v_own, v_off, v_par = lax.switch(code // 2, branches, orbitals, other)
+    return pairs(kernel_rates, kernel_weights, orbitals, off, par, v_own, v_off, v_par)
 
 
 def solution(mesh):

time: 167 us -> 160 us (0.958)
  the two profiles are of different devices: /device:TPU:3 before, /device:TPU:4 now
where the time goes in v1:
time: 160 us
  Pallas kernels  155 us (97%)
  local copies, waits for them, and re-layouts  2.41 us (2%)
  between operations  1.85 us (1%)
    pallas_call x1, Pallas kernels, exchange(): pl.pallas_call(functools.partial(exchange_kernel, owner), out_shape=[jax....  131 us
    pallas_call x1, Pallas kernels, pairs(): pl.pallas_call(pair_kernel, out_shape=jax.ShapeDtypeStruct(blocks[0].shap...  23.8 us

profile of v1, /device:TPU:4, one launch (start us, length us, event | category | flops | bytes accessed | tf_op | source)
XLA Modules:
  0.0 159.8 jit_solution(10678876953776141501)
XLA Ops:
  0.0 1.3 fusion
  3.1 1.1 constant_dynamic-slice_fusion
  4.2 0.0 copy-start
  4.2 0.0 copy-start.1
  4.2 131.8 %conditional.1 = ((bf16[8,2,128,256]{3,2,1,0:T(8,128)(2,1)S(1)}, bf16[8,2,128,256]{3,2,1,0:T(8,128)(2,1)S(1)}, bf16[8,2,128,256]{3,2,1,0:T(8,128)(2,1)S(1)}, bf1...) conditional(s32[]{:T(128)} %clamp.3, (bf16[8,2,128,256]{3,2,1,0:T(8,128)(2,1)}, ...), branch_computations={%region_0.1_spmd, %region_1.2_spmd, %region_2.3_spmd, %region_3.4_... | conditional | bytes 8 | solution.py:273
  4.3 131.3 %exchange4.1 = (bf16[8,2,128,256]{3,2,1,0:T(8,128)(2,1)S(1)}, bf16[8,2,128,256]{3,2,1,0:T(8,128)(2,1)S(1)}, bf16[8,2,128,256]{3,2,1,0:T(8,128)(2,1)S(1)}, bf16[8...) custom-call(bf16[8,2,128,256]{3,2,1,0:T(8,128)(2,1)} %get-tuple-element.45.orbitals, ...), custom_call_target="tpu_custom_call" | custom-call | tf_op jit(solution)/shard_map/cond/branch_4_fun/exchange4/pallas_call | solution.py:256
  136.0 0.0 copy-done
  136.0 0.0 copy-done.1
  136.0 23.8 %shard_map.46 = f32[8,2,128,256]{3,2,1,0:T(8,128)} custom-call(f32[3]{0:T(128)S(1)} %copy-done, f32[3]{0:T(128)S(1)} %copy-done.1, bf16[8,2,128,256]{3,2,1,0:T(8,128)(2,1)} %own.1, bf16[8,2,128,256]{3,2,1,0:T(8,128)(2,1)S(1)} %get-tuple-element.58.off, bf16[8,2,128,256]{3,2,1,0:T(8,128)(2,1)S(1)} %get-tuple-element.59.par, ...), custom_call_target="tpu_custom_call" | custom-call | tf_op jit(solution)/shard_map/pallas_call | solution.py:92
Async XLA Ops:
  4.2 131.8 %copy-start = (f32[3]{0:T(128)S(1)}, f32[3]{0:T(128)}, u32[]{:S(2)}) copy-start(f32[3]{0:T(128)} %rates.1) | copy-start | bytes 40
  4.2 131.8 %copy-start.1 = (f32[3]{0:T(128)S(1)}, f32[3]{0:T(128)}, u32[]{:S(2)}) copy-start(f32[3]{0:T(128)} %weights.1) | copy-start | bytes 40

commit v2 on v1

--- a/solution.py
+++ b/solution.py
@@ -15,6 +15,7 @@
 LAST_OWNER = 7
 CROSS = (0, 1, 3, 2)
 EARLY = 2
+TURNS = 10
 MESH = pl.DeviceIdType.MESH
 CHUNK = 16
 
@@ -151,6 +152,13 @@
         far_down = jnp.logical_not(home) & (step == 0 if not halo else (step == 0) | (step == 3))
         go_up = far_up if go_up is None else go_up | far_up
         go_down = far_down if go_down is None else go_down | far_down
+        if climbs:
+            depth = gap
+        else:
+            depth = (RING - gap) % RING
+        spread = jnp.where(step == 0, 0, jnp.where(step == 2, 2, 1))
+        depth = jnp.where(home, depth, (0, 1, 1, 2)[m] + 1 + spread)
+        turn = depth + m % 2 + 3 * halo
         buffer, recv = (v_off, off_recv) if halo else (v_own, own_recv)
         slots = unit_send.at[halo, row]
         first = band == root
@@ -171,7 +179,7 @@
             plan.append((first, send(source, v_par.at[row], slots.at[3], par_recv.at[row], dom=mate)))
             plan.append((jnp.logical_not(first), send(v_own.at[row], v_par.at[row], slots.at[3], par_recv.at[row], dom=mate)))
             plan.append((first & inside, send(source, v_off.at[row], slots.at[4], off_recv.at[row], dom=away)))
-        return first, source, row, plan
+        return first, source, row, plan, turn
 
     def start(condition, copy):
         @pl.when(condition)
@@ -188,16 +196,14 @@
     units = [(block, m, halo) for halo in range(2) for m in (0, 2, 1, 3) for block in range(2)]
     plans = [routes(*unit) for unit in units]
 
-    for (block, m, halo), (first, source, row, plan) in zip(units, plans):
-        if not halo:
-            for condition, copy in plan:
-                pass
+    for (block, m, halo), (first, source, row, plan, turn) in zip(units, plans):
+        if not halo:
 
             @pl.when(first)
             def _(source=source, row=row):
                 pltpu.make_async_copy(source, v_own.at[row], local_sem.at[row]).start()
 
-    for (block, m, halo), (first, source, row, plan) in zip(units, plans):
+    for (block, m, halo), (first, source, row, plan, turn) in zip(units, plans):
         if not halo:
 
             @pl.when(first)
@@ -209,27 +215,26 @@
         start(inside, r_away[i])
     for copy in r_mate:
         copy.start()
-    waiting = list(r_away[EARLY:])
-    for (block, m, halo), (first, source, row, plan) in zip(units, plans):
-        if halo:
-
-            @pl.when(inside)
-            def _(row=row):
-                send(v_off.at[row], v_off.at[row], unit_send.at[1, row, 4], off_recv.at[row], dom=away).wait_recv()
-
-            for condition, copy in plan:
-                start(condition, copy)
-        else:
-
-            @pl.when(jnp.logical_not(first))
-            def _(row=row, plan=plan):
-                send(v_own.at[row], v_own.at[row], unit_send.at[0, row, 0], own_recv.at[row], dom=mate).wait_recv()
+    def advance(now, carry):
+        for (block, m, halo), (first, source, row, plan, turn) in zip(units, plans):
+            arrives = inside if halo else jnp.logical_not(first)
+
+            @pl.when(arrives & (turn == now))
+            def _(halo=halo, row=row, plan=plan):
+                buffer, recv = (v_off, off_recv) if halo else (v_own, own_recv)
+                send(buffer.at[row], buffer.at[row], unit_send.at[halo, row, 0], recv.at[row], dom=mate).wait_recv()
                 for condition, copy in plan:
                     start(condition, copy)
 
-        if waiting:
-            start(inside, waiting.pop(0))
-    for (block, m, halo), (first, source, row, plan) in zip(units, plans):
+        @pl.when(inside & (now < 2 * BLOCK - EARLY))
+        def _():
+            i = EARLY + now
+            send(orbitals.at[i], off.at[i], r_send.at[0, i], r_off_recv.at[i], dom=away).start()
+
+        return carry
+
+    lax.fori_loop(0, TURNS, advance, 0)
+    for (block, m, halo), (first, source, row, plan, turn) in zip(units, plans):
         for condition, copy in plan:
             finish(condition, copy)
         if not halo:

time: 160 us -> 96.3 us (0.60)
  Pallas kernels: 155 us -> 91.5 us
    pallas_call x1, Pallas kernels: 131 us -> 67.7 us  [exchange(): pl.pallas_call(functools.partial(exchange_kernel, owner), out_shape=[jax....]
where the time goes in v2:
time: 96.3 us; the launch traced here: 96.1 us
  Pallas kernels  91.5 us (95%)
  local copies, waits for them, and re-layouts  2.41 us (3%)
  between operations  1.85 us (2%)
    pallas_call x1, Pallas kernels, exchange(): pl.pallas_call(functools.partial(exchange_kernel, owner), out_shape=[jax....  67.7 us
    pallas_call x1, Pallas kernels, pairs(): pl.pallas_call(pair_kernel, out_shape=jax.ShapeDtypeStruct(blocks[0].shap...  23.8 us

profile of v2, /device:TPU:4, one launch (start us, length us, event | category | flops | bytes accessed | tf_op | source)
XLA Modules:
  0.0 96.1 jit_solution(9502364929116562710)
XLA Ops:
  0.0 1.3 %fusion = (s32[1]{0:T(128)}, s32[1]{0:T(128)}) fusion(s32[2]{0:T(128)} %param.13), kind=kLoop, calls=%fused_computation.1 | loop fusion | bytes 16 | tf_op jit(solution)/shard_map/slice | solution.py:275
  3.1 1.1 %constant_dynamic-slice_fusion = bf16[4,2,128,256]{3,2,1,0:T(8,128)(2,1)S(1)} fusion(bf16[8,2,128,256]{3,2,1,0:T(8,128)(2,1)} %own.1, s32[]{:T(128)S(6)} %select_n.20), kind=kLoop, calls=%fused_computation | loop fusion | bytes 1048580 | tf_op jit(solution)/shard_map/dynamic_slice | solution.py:276
  4.2 0.0 copy-start
  4.2 0.0 copy-start.1
  4.2 68.0 %conditional.1 = ((bf16[8,2,128,256]{3,2,1,0:T(8,128)(2,1)S(1)}, bf16[8,2,128,256]{3,2,1,0:T(8,128)(2,1)S(1)}, bf16[8,2,128,256]{3,2,1,0:T(8,128)(2,1)S(1)}, bf1...) conditional(s32[]{:T(128)} %clamp.3, (bf16[8,2,128,256]{3,2,1,0:T(8,128)(2,1)}, ...), branch_computations={%region_0.1_spmd, %region_1.2_spmd, %region_2.3_spmd, %region_3.4_... | conditional | bytes 8 | solution.py:278
  4.3 67.7 %exchange0.1 = (bf16[8,2,128,256]{3,2,1,0:T(8,128)(2,1)S(1)}, bf16[8,2,128,256]{3,2,1,0:T(8,128)(2,1)S(1)}, bf16[8,2,128,256]{3,2,1,0:T(8,128)(2,1)S(1)}, bf16[8...) custom-call(bf16[8,2,128,256]{3,2,1,0:T(8,128)(2,1)} %get-tuple-element.37.orbitals, ...), custom_call_target="tpu_custom_call" | custom-call | tf_op jit(solution)/shard_map/cond/branch_0_fun/exchange0/pallas_call | solution.py:261
  72.2 0.0 copy-done
  72.2 0.0 copy-done.1
  72.3 23.8 %shard_map.46 = f32[8,2,128,256]{3,2,1,0:T(8,128)} custom-call(f32[3]{0:T(128)S(1)} %copy-done, f32[3]{0:T(128)S(1)} %copy-done.1, bf16[8,2,128,256]{3,2,1,0:T(8,128)(2,1)} %own.1, bf16[8,2,128,256]{3,2,1,0:T(8,128)(2,1)S(1)} %get-tuple-element.58.off, bf16[8,2,128,256]{3,2,1,0:T(8,128)(2,1)S(1)} %get-tuple-element.59.par, ...), custom_call_target="tpu_custom_call" | custom-call | tf_op jit(solution)/shard_map/pallas_call | solution.py:93
Async XLA Ops:
  4.2 68.0 %copy-start = (f32[3]{0:T(128)S(1)}, f32[3]{0:T(128)}, u32[]{:S(2)}) copy-start(f32[3]{0:T(128)} %rates.1) | copy-start | bytes 40
  4.2 68.0 %copy-start.1 = (f32[3]{0:T(128)S(1)}, f32[3]{0:T(128)}, u32[]{:S(2)}) copy-start(f32[3]{0:T(128)} %weights.1) | copy-start | bytes 40

commit v3 on v2

--- a/solution.py
+++ b/solution.py
@@ -13,9 +13,42 @@
 GAUSS = 3
 RING = 4
 LAST_OWNER = 7
-CROSS = (0, 1, 3, 2)
-EARLY = 2
-TURNS = 10
+EARLY = 0
+TURNS = 16
+SCHEDULES = (
+    (
+        (10524161, 106601, 7864528, 45133, 4915226, 2364802, 14685824, 6818946, 5833408, 45071, 6833155, 106601, 15205889, 6817803, 10524288, 4206607),
+        (67114086, 3072741376, 269644379, 3643908881, 558431101, 2783772978, 844314537, 2329683331, 1131137231, 2608154148, 1451548634, 4238272837, 1756859132, 3456068759, 2143993326, 4004093624),
+    ),
+    (
+        (5832912, 4207638, 2150411, 361522, 15206016, 852808, 13174273, 106616, 10524161, 2392680, 2151427, 852808, 7344336, 4206622, 15206016, 106554),
+        (1401482, 2321683712, 354450835, 2734901521, 557908900, 2492211237, 844707831, 3073855794, 1284803769, 3380515916, 1589047259, 3958359646, 1725496271, 3757811814, 2026553069, 4256029304),
+    ),
+    (
+        (2151427, 852801, 6426712, 2884417, 13174400, 45206, 14685328, 106736, 10523145, 106674, 2151427, 6818369, 5833408, 2884048, 14685824, 2884048),
+        (83921490, 1628700720, 270662763, 2489983365, 574035827, 2930070017, 861030846, 3645453076, 1265860297, 4253795366, 1606873066, 3170657703, 1990056927, 3351156296, 2296954364, 3940526237),
+    ),
+    (
+        (2150411, 4787344, 2150411, 45581, 7864528, 853392, 5833281, 46597, 2150411, 6818313, 5833408, 2885008, 14685697, 4208260, 14685824, 6819456),
+        (50366786, 1112080388, 371309957, 2840794128, 538088282, 3026985255, 825738989, 3734319665, 1551167417, 2614840419, 1703869135, 3938407804, 2007411675, 4293552022, 2294865662, 3455940776),
+    ),
+    (
+        (10524288, 430106, 10524161, 430168, 5832912, 4744195, 7864528, 4743179, 10524288, 4743179, 2150411, 176216, 10524288, 13116929, 7865024, 4744195),
+        (104071201, 2986369539, 408228708, 3557926454, 539771225, 1130505488, 826836092, 1434671170, 1822111655, 2848365973, 2126376923, 3396860813, 2413722346, 3957964030, 2544884175, 4261072568),
+    ),
+    (
+        (10524161, 491546, 2150411, 4399130, 7865024, 10782336, 15205889, 1409232, 13174400, 2523224, 2151427, 4284427, 5833408, 4399192, 15206016, 237656),
+        (139460640, 1342251265, 445798738, 2568192787, 560218696, 2183817963, 866522228, 3023402380, 1171077014, 3327039029, 1860755418, 3715612343, 2011154639, 4018793321, 2885463293, 4240178606),
+    ),
+    (
+        (10524161, 868363, 2265176, 3412176, 7344832, 983066, 13174273, 615427, 13174400, 3412176, 6311947, 10753664, 5832912, 983066, 14685697, 1900752),
+        (186646816, 1073896017, 490850119, 1367678980, 610484792, 2182382611, 894966642, 3812015781, 1790850454, 3068883821, 2091380681, 3355286780, 2665470430, 3631938955, 2949212394, 4187793087),
+    ),
+    (
+        (2265176, 2151427, 10524161, 2150411, 2150411, 5832912, 4915288, 5833408, 2151427, 10524288, 10524161, 4915288, 5832912, 5832912, 15206016, 15205889),
+        (50365444, 354497841, 658636816, 962820707, 1267056311, 1343496485, 1630979912, 1918390873, 2376589274, 2663977842, 2951432358, 3027958924, 3332150941, 3636390351, 3940379627, 4244614654),
+    ),
+)
 MESH = pl.DeviceIdType.MESH
 CHUNK = 16
 
@@ -137,35 +170,25 @@
             src_ref=source, dst_ref=target, send_sem=send_sem, recv_sem=recv_sem, device_id=device, device_id_type=MESH
         )
 
+    def by_band(packed, base):
+        value = 0
+        for k in range(lax.axis_size("band")):
+            value = jnp.where(band == k, packed // base**k % base, value)
+        return value
+
     def routes(block, m, halo):
         root = (LAST_OWNER, owner)[block]
         row = block * BLOCK + m
-        gap = (place + RING - root % RING) % RING
-        home = side == root // RING
-        step = (gap - CROSS[m] + RING) % RING
-        climbs = m < BLOCK // 2
-        if climbs:
-            go_up, go_down = home & (gap < 3), None
-        else:
-            go_up, go_down = None, home & (gap != 1)
-        far_up = jnp.logical_not(home) & ((step == 0) | (step == 1) if not halo else step == 0)
-        far_down = jnp.logical_not(home) & (step == 0 if not halo else (step == 0) | (step == 3))
-        go_up = far_up if go_up is None else go_up | far_up
-        go_down = far_down if go_down is None else go_down | far_down
-        if climbs:
-            depth = gap
-        else:
-            depth = (RING - gap) % RING
-        spread = jnp.where(step == 0, 0, jnp.where(step == 2, 2, 1))
-        depth = jnp.where(home, depth, (0, 1, 1, 2)[m] + 1 + spread)
-        turn = depth + m % 2 + 3 * halo
+        number = (halo * BLOCK + m) * 2 + block
+        flags = by_band(SCHEDULES[owner][0][number], 8)
+        turn = by_band(SCHEDULES[owner][1][number], 16)
         buffer, recv = (v_off, off_recv) if halo else (v_own, own_recv)
         slots = unit_send.at[halo, row]
         first = band == root
         source = orbitals.at[BLOCK + m] if block == 0 else other.at[m]
         plan = []
         for k, (condition, device) in enumerate(
-            ((go_up, {"band": up}), (go_down, {"band": down}), (home & (gap == CROSS[m]), {"band": twin}))
+            ((flags % 2 == 1, {"band": up}), (flags // 2 % 2 == 1, {"band": down}), (flags // 4 == 1, {"band": twin}))
         ):
             if halo:
                 condition = condition & inside
@@ -193,7 +216,7 @@
 
     r_away = [send(orbitals.at[i], off.at[i], r_send.at[0, i], r_off_recv.at[i], dom=away) for i in range(2 * BLOCK)]
     r_mate = [send(orbitals.at[i], par.at[i], r_send.at[1, i], r_par_recv.at[i], dom=mate) for i in range(2 * BLOCK)]
-    units = [(block, m, halo) for halo in range(2) for m in (0, 2, 1, 3) for block in range(2)]
+    units = [(block, m, halo) for halo in range(2) for m in range(BLOCK) for block in range(2)]
     plans = [routes(*unit) for unit in units]
 
     for (block, m, halo), (first, source, row, plan, turn) in zip(units, plans):
@@ -208,7 +231,7 @@
 
             @pl.when(first)
             def _(plan=plan):
-                for condition, copy in plan:
+                for condition, copy in plan[6:]:
                     start(condition, copy)
 
     for i in range(EARLY):
@@ -219,12 +242,18 @@
         for (block, m, halo), (first, source, row, plan, turn) in zip(units, plans):
             arrives = inside if halo else jnp.logical_not(first)
 
-            @pl.when(arrives & (turn == now))
-            def _(halo=halo, row=row, plan=plan):
+            @pl.when(turn == now)
+            def _(halo=halo, row=row, plan=plan, arrives=arrives):
                 buffer, recv = (v_off, off_recv) if halo else (v_own, own_recv)
-                send(buffer.at[row], buffer.at[row], unit_send.at[halo, row, 0], recv.at[row], dom=mate).wait_recv()
-                for condition, copy in plan:
+
+                @pl.when(arrives)
+                def _():
+                    send(buffer.at[row], buffer.at[row], unit_send.at[halo, row, 0], recv.at[row], dom=mate).wait_recv()
+
+                for condition, copy in plan if halo else plan[:6]:
                     start(condition, copy)
+                if not halo:
+                    start(*plan[7])
 
         @pl.when(inside & (now < 2 * BLOCK - EARLY))
         def _():

time: 96.3 us -> 89.8 us (0.933)
  the two profiles are of different devices: /device:TPU:4 before, /device:TPU:50 now
where the time goes in v3:
time: 89.8 us; the launch traced here: 88.2 us
  Pallas kernels  83.7 us (93%)
  local copies, waits for them, and re-layouts  2.41 us (3%)
  between operations  1.85 us (2%)
    pallas_call x1, Pallas kernels, exchange(): pl.pallas_call(functools.partial(exchange_kernel, owner), out_shape=[jax....  59.9 us
    pallas_call x1, Pallas kernels, pairs(): pl.pallas_call(pair_kernel, out_shape=jax.ShapeDtypeStruct(blocks[0].shap...  23.8 us

profile of v3, /device:TPU:50, one launch (start us, length us, event | category | flops | bytes accessed | tf_op | source)
XLA Modules:
  0.0 88.2 jit_solution(1946152463379171766)
XLA Ops:
  0.0 1.3 %fusion = (s32[1]{0:T(128)}, s32[1]{0:T(128)}) fusion(s32[2]{0:T(128)} %param.13), kind=kLoop, calls=%fused_computation.1 | loop fusion | bytes 16 | tf_op jit(solution)/shard_map/slice | solution.py:304
  3.1 1.1 %constant_dynamic-slice_fusion = bf16[4,2,128,256]{3,2,1,0:T(8,128)(2,1)S(1)} fusion(bf16[8,2,128,256]{3,2,1,0:T(8,128)(2,1)} %own.1, s32[]{:T(128)S(6)} %select_n.20), kind=kLoop, calls=%fused_computation | loop fusion | bytes 1048580 | tf_op jit(solution)/shard_map/dynamic_slice | solution.py:305
  4.2 0.0 copy-start
  4.2 0.0 copy-start.1
  4.2 60.1 %conditional.1 = ((bf16[8,2,128,256]{3,2,1,0:T(8,128)(2,1)S(1)}, bf16[8,2,128,256]{3,2,1,0:T(8,128)(2,1)S(1)}, bf16[8,2,128,256]{3,2,1,0:T(8,128)(2,1)S(1)}, bf1...) conditional(s32[]{:T(128)} %clamp.3, (bf16[8,2,128,256]{3,2,1,0:T(8,128)(2,1)}, ...), branch_computations={%region_0.1_spmd, %region_1.2_spmd, %region_2.3_spmd, %region_3.4_... | conditional | bytes 8 | solution.py:307
  4.3 59.9 %exchange0.1 = (bf16[8,2,128,256]{3,2,1,0:T(8,128)(2,1)S(1)}, bf16[8,2,128,256]{3,2,1,0:T(8,128)(2,1)S(1)}, bf16[8,2,128,256]{3,2,1,0:T(8,128)(2,1)S(1)}, bf16[8...) custom-call(bf16[8,2,128,256]{3,2,1,0:T(8,128)(2,1)} %get-tuple-element.37.orbitals, ...), custom_call_target="tpu_custom_call" | custom-call | tf_op jit(solution)/shard_map/cond/branch_0_fun/exchange0/pallas_call | solution.py:290
  64.3 0.0 copy-done
  64.3 0.0 copy-done.1
  64.3 23.8 %shard_map.46 = f32[8,2,128,256]{3,2,1,0:T(8,128)} custom-call(f32[3]{0:T(128)S(1)} %copy-done, f32[3]{0:T(128)S(1)} %copy-done.1, bf16[8,2,128,256]{3,2,1,0:T(8,128)(2,1)} %own.1, bf16[8,2,128,256]{3,2,1,0:T(8,128)(2,1)S(1)} %get-tuple-element.58.off, bf16[8,2,128,256]{3,2,1,0:T(8,128)(2,1)S(1)} %get-tuple-element.59.par, ...), custom_call_target="tpu_custom_call" | custom-call | tf_op jit(solution)/shard_map/pallas_call | solution.py:126
Async XLA Ops:
  4.2 60.1 %copy-start = (f32[3]{0:T(128)S(1)}, f32[3]{0:T(128)}, u32[]{:S(2)}) copy-start(f32[3]{0:T(128)} %rates.1) | copy-start | bytes 40
  4.2 60.1 %copy-start.1 = (f32[3]{0:T(128)S(1)}, f32[3]{0:T(128)}, u32[]{:S(2)}) copy-start(f32[3]{0:T(128)} %weights.1) | copy-start | bytes 40
